TPU v7x, 128 devices: a whole 4x4x4 slice. The times are simulated.
128 devices in a mesh: ctx: 8 (over y_hi, x), exp: 16 (over y_lo, z, core).
Axes of the slice: x: 4, y: 4 (y_hi: 2, y_lo: 2; y = y_hi * 2 + y_lo), z: 4, core: 2. Of those that a mesh axis runs over, the one named last changes fastest.
Arguments:
- queries: bfloat16 [16, 1024, 2048], P('exp', 'ctx'), may hold values from -6 to 6
- key_rows: bfloat16 [16, 1024, 256], P('exp', 'ctx'), may hold values from -6 to 6
- value_matrix: bfloat16 [16, 1024, 256], P('exp', 'ctx'), may hold values from -4 to 4
- hidden: bfloat16 [16, 1024, 2880], P('exp', 'ctx'), may hold values from -30 to 30
- out_weight: bfloat16 [2048, 2880], P('ctx'), may hold values from -0.125 to 0.125
- norm_gain: float32 [2880], replicated, may hold values from 0.1 to 1.9
- block_order: int32 [16], replicated, may hold values from 0 to 15, each once
- expert_ids: int32 [16, 1024, 4], P('exp', 'ctx'), may hold values from 0 to 63, all different within a row; in each aligned block of 128 rows (0 to 127, 128 to 255, ..., all dimensions but the last counted through in order) at most 16 rows name the same one
- route_weights: float32 [16, 1024, 4], P('exp', 'ctx'), may hold values from 0.1 to 0.6
- gate_up_weight: bfloat16 [128, 2880, 1440], P(('ctx', 'exp')), may hold values from -0.109375 to 0.109375
- down_weight: bfloat16 [128, 720, 2880], P(('ctx', 'exp')), may hold values from -0.15625 to 0.15625
Outputs:
- layer_out: bfloat16 [16, 1024, 2880], P('exp', 'ctx')
Inputs may be any that keep to these rules, and one draw needn't show every extreme that they name: `expert_ids`: the 128 rows of one device (aligned blocks of rows) name any one expert at most 16 times, a bound that some block reaches.
All inputs are finite; a program needn't handle non-finite values.
Results may differ from a plain program's by a relative error of at most 0.017.
Values may be sent and summed in bfloat16 or wider, within the bound.
A program may use at most 128 MiB of HBM per device.

v0:
```python
import jax
import jax.numpy as jnp
from jax import lax
from jax.sharding import PartitionSpec as P

D = 2880
QUERY_HEADS = 32
KEY_VALUE_HEADS = 4
HEAD_SIZE = 64
TOPK = 4
negative_large = -1e30


def expert_half(routed, gate_up, down_part):
    half_size = gate_up.shape[1] // 2
    gate_up_out = jnp.dot(routed, gate_up, preferred_element_type=jnp.float32)
    gate_part = gate_up_out[:, :half_size]
    up_part = gate_up_out[:, half_size:]
    activated = (gate_part * jax.nn.sigmoid(1.702 * gate_part) * (up_part + 1.0)).astype(
        jnp.bfloat16
    )
    return jnp.dot(activated, down_part, preferred_element_type=jnp.float32).astype(jnp.bfloat16)


def local(
    queries,
    key_rows,
    value_matrix,
    hidden,
    out_weight,
    norm_gain,
    block_order,
    expert_ids,
    route_weights,
    gate_up_weight,
    down_weight,
):
    ctx_count = lax.axis_size("ctx")
    exp_count = lax.axis_size("exp")
    token_count = queries.shape[1]
    block_len = token_count // 2
    query_group_size = QUERY_HEADS // KEY_VALUE_HEADS
    slot_ids = jnp.arange(2 * ctx_count, dtype=jnp.int32)

    def locate(row_index):
        table = (row_index // block_len)[:, None] == slot_ids[None, :]
        return (
            jnp.sum(jnp.where(table, block_order[None, :], 0), axis=1) * block_len
            + row_index % block_len
        )

    query_pos = locate(
        lax.axis_index("ctx") * token_count + jnp.arange(token_count, dtype=jnp.int32)
    )
    query_head_rows = queries[0].reshape(token_count, KEY_VALUE_HEADS, query_group_size, HEAD_SIZE)
    key_section = lax.all_gather(key_rows, "ctx", axis=1, tiled=True)
    value_section = lax.all_gather(value_matrix, "ctx", axis=1, tiled=True)
    section_length = key_section.shape[1]
    key_pos = locate(jnp.arange(section_length, dtype=jnp.int32))
    row_maximum = jnp.full(
        (KEY_VALUE_HEADS, query_group_size, token_count), negative_large, jnp.float32
    )
    key_head_rows = key_section[0].reshape(section_length, KEY_VALUE_HEADS, HEAD_SIZE)
    value_head_rows = value_section[0].reshape(section_length, KEY_VALUE_HEADS, HEAD_SIZE)
    scores = jnp.einsum(
        "qhgd,khd->hgqk", query_head_rows, key_head_rows, preferred_element_type=jnp.float32
    ) * HEAD_SIZE ** (-0.5)
    visible = key_pos[None, :] <= query_pos[:, None]
    masked = jnp.where(visible, scores, negative_large)
    new_max = jnp.maximum(row_maximum, jnp.max(masked, axis=-1))
    kept_probs = jnp.where(visible, jnp.exp(masked - new_max[..., None]), 0.0)
    row_total = jnp.sum(kept_probs, axis=-1)
    added = jnp.einsum(
        "hgqk,khd->qhgd",
        kept_probs.astype(jnp.bfloat16),
        value_head_rows,
        preferred_element_type=jnp.float32,
    )
    weighted_sum = added
    row_maximum, row_total, weighted_sum = (new_max, row_total, weighted_sum)
    attended = (
        (weighted_sum / jnp.transpose(row_total, (2, 0, 1))[..., None])
        .astype(jnp.bfloat16)
        .reshape(token_count, QUERY_HEADS * HEAD_SIZE)
    )
    projected = jnp.dot(
        attended,
        lax.all_gather(out_weight, "ctx", axis=0, tiled=True),
        preferred_element_type=jnp.float32,
    )
    residual = (hidden[0].astype(jnp.float32) + projected).astype(jnp.bfloat16)
    res_float = residual.astype(jnp.float32)
    moe_in = (
        res_float
        * lax.rsqrt(jnp.mean(res_float * res_float, axis=-1, keepdims=True) + 1e-05)
        * norm_gain
    ).astype(jnp.bfloat16)
    device_count = ctx_count * exp_count
    experts = device_count // 2
    capacity = 2 * token_count * TOPK // experts
    flat_ids = expert_ids[0].reshape(-1)
    onehot = (flat_ids[:, None] == jnp.arange(experts, dtype=jnp.int32)[None, :]).astype(jnp.int32)
    slot_index = jnp.sum((jnp.cumsum(onehot, axis=0) - 1) * onehot, axis=1)
    copies = jnp.repeat(moe_in, TOPK, axis=0)
    outgoing = jnp.zeros((experts, capacity, D), jnp.bfloat16).at[flat_ids, slot_index].set(copies)
    gate_up_local = gate_up_weight[0]
    down_local = down_weight[0]
    doubled = jnp.broadcast_to(outgoing[:, None], (experts, 2, capacity, D)).reshape(
        device_count, capacity, D
    )
    batch_rows = lax.all_to_all(doubled, ("ctx", "exp"), split_axis=0, concat_axis=0, tiled=True)
    flat_rows = batch_rows.reshape(-1, D)
    returned = lax.all_to_all(
        expert_half(flat_rows, gate_up_local, down_local).reshape(batch_rows.shape),
        ("ctx", "exp"),
        split_axis=0,
        concat_axis=0,
        tiled=True,
    )
    paired = returned.reshape(experts, 2, capacity, D)[flat_ids, :, slot_index]
    summed = (
        (paired[:, 0].astype(jnp.float32) + paired[:, 1].astype(jnp.float32))
        .astype(jnp.bfloat16)
        .astype(jnp.float32)
    )
    mixed = (
        (summed * route_weights[0].reshape(-1)[:, None]).reshape(token_count, TOPK, D).sum(axis=1)
    )
    return (res_float + mixed).astype(jnp.bfloat16)[None]


def solution(mesh):
    return jax.shard_map(
        local,
        mesh=mesh,
        in_specs=(
            P("exp", "ctx", None),
            P("exp", "ctx", None),
            P("exp", "ctx", None),
            P("exp", "ctx", None),
            P("ctx", None),
            P(),
            P(),
            P("exp", "ctx", None),
            P("exp", "ctx", None),
            P(("ctx", "exp"), None, None),
            P(("ctx", "exp"), None, None),
        ),
        out_specs=P("exp", "ctx", None),
        check_vma=False,
    )
```

profile of v0, /device:TPU:36, one launch (start us, length us, event | category | flops | bytes accessed | tf_op | source)
XLA Modules:
  0.0 783.1 jit_solution(11252463984967815645)
XLA Ops:
  8.4 34.9 %all_gather.9 = bf16[1,1024,256]{2,1,0:T(8,128)(2,1)S(1)} all-gather(bf16[1,128,256]{2,1,0:T(8,128)(2,1)} %param.12), channel_id=1, replica_groups=mesh['ctx'=8,'exp'=16] {'ctx'}, dimensions={1}, use_global_device_ids=true | all-gather | bytes 589824 | tf_op jit(solution)/shard_map/all_gather | solution.py:56
  44.9 36.4 %all_gather.10 = bf16[1,1024,256]{2,1,0:T(8,128)(2,1)S(1)} all-gather(bf16[1,128,256]{2,1,0:T(8,128)(2,1)} %param.13), channel_id=1, replica_groups=mesh['ctx'=8,'exp'=16] {'ctx'}, dimensions={1}, use_global_device_ids=true | all-gather | bytes 589824 | tf_op jit(solution)/shard_map/all_gather | solution.py:57
  84.1 2.4 fusion
  86.5 4.3 fusion.1
  90.8 4.0 divide_convert_fusion
  94.8 76.3 %all-gather.2.cloned.1.call-done = bf16[2048,2880]{0,1:T(8,128)(2,1)} async-done(((bf16[256,2880]{0,1:T(8,128)(2,1)}), bf16[2048,2880]{0,1:T(8,128)(2,1)}) %all-gather.2.cloned.1.call-update) | async-done | bytes 11796496 | tf_op jit(solution)/shard_map/all_gather | solution.py:88
  171.1 6.2 multiply_reduce_fusion.1
  179.3 2.4 broadcast_in_dim.80
  181.7 4.4 reshape.192
  186.1 3.0 broadcast_in_dim.79
  189.0 107.0 %scatter_fusion = bf16[64,16,2880]{2,1,0:T(8,128)(2,1)} fusion(bf16[64,16,2880]{2,1,0:T(8,128)(2,1)} %broadcast_in_dim.79, s32[512]{0:T(512)S(1)} %bitcast.74, bf16[512,2880]{1,0:T(8,128)(2,1)S(1)} %reshape.192), kind=kCustom, calls=%fused_computation.1 | custom fusion | bytes 8851456 | tf_op jit(solution)/shard_map/scatter | solution.py:105
  296.0 5.4 broadcast_in_dim.81
  301.4 146.1 %all_to_all.10 = bf16[128,16,2880]{2,1,0:T(8,128)(2,1)S(1)} all-to-all(bf16[128,16,2880]{2,1,0:T(8,128)(2,1)S(1)} %bitcast.73), channel_id=1, replica_groups=mesh['ctx'=8,'exp'=16] {'ctx','exp'}, dimensions={0} | all-to-all | bytes 23592960 | tf_op jit(solution)/shard_map/all_to_all | solution.py:111
  447.5 21.1 %fusion.3 = f32[2048,1440]{0,1:T(8,128)} fusion(bf16[2048,2880]{1,0:T(8,128)(2,1)S(1)} %bitcast.76, bf16[1,2880,1440]{1,2,0:T(8,128)(2,1)S(1)} %bitcast.84), kind=kOutput, calls=%fused_computation.8 | convolution fusion | flops 16986931200 | bytes 31887360 | tf_op jit(solution)/shard_map/dot_general | solution.py:16
  468.7 17.1 %convolution_convert_fusion = bf16[2048,2880]{0,1:T(8,128)(2,1)} fusion(bf16[1,720,2880]{2,1,0:T(8,128)(2,1)S(1)} %bitcast.86, f32[2048,1440]{0,1:T(8,128)} %fusion.3), kind=kOutput, calls=%fused_computation.7 | convolution fusion | flops 8511160320 | bytes 27740160 | tf_op jit(solution)/shard_map/dot_general | solution.py:22
  485.8 16.3 %copy.63 = bf16[2048,2880]{1,0:T(8,128)(2,1)} copy(bf16[2048,2880]{0,1:T(8,128)(2,1)} %convolution_convert_fusion) | data formatting | bytes 23592960 | tf_op jit(solution)/shard_map/convert_element_type | solution.py:22
  502.1 16.2 %all-to-all-start.1 = ((bf16[128,16,2880]{2,1,0:T(8,128)(2,1)}), bf16[128,16,2880]{2,1,0:T(8,128)(2,1)}, u32[]{:S(2)}, u32[]{:S(2)}) async-start(bf16[128,16,2880]{2,1,0:T(8,128)(2,1)} %bitcast.72), calls=%async_computation.1 | async-start | bytes 24117248 | tf_op jit(solution)/shard_map/all_to_all | solution.py:113
  518.5 172.9 %all-to-all-done.1 = bf16[128,16,2880]{2,1,0:T(8,128)(2,1)} async-done(((bf16[128,16,2880]{2,1,0:T(8,128)(2,1)}), bf16[128,16,2880]{2,1,0:T(8,128)(2,1)}, u32[]{:S(2)}, u32[]{:S(2)}) %all-to-all-start.1) | async-done | bytes 11796512 | tf_op jit(solution)/shard_map/all_to_all | solution.py:113
  691.4 18.0 %copy.64 = bf16[64,2,16,2880]{3,1,2,0:T(2,128)(2,1)} copy(bf16[64,2,16,2880]{3,2,1,0:T(8,128)(2,1)} %bitcast.20) | data formatting | bytes 23592960 | tf_op jit(solution)/shard_map/reshape | solution.py:120
  709.4 22.0 %gather_fusion = bf16[512,2,2880]{2,1,0:T(2,128)(2,1)} fusion(bf16[64,2,16,2880]{3,1,2,0:T(2,128)(2,1)} %copy.64, s32[512]{0:T(512)S(1)} %bitcast.75), kind=kCustom, calls=%fused_computation | custom fusion | bytes 11800576 | tf_op jit(solution)/shard_map/gather | solution.py:120
  731.4 26.1 %fusion.11 = f32[512,2880]{1,0:T(8,128)} fusion(bf16[512,2,2880]{2,1,0:T(2,128)(2,1)} %gather_fusion), kind=kLoop, calls=%fused_computation.16 | loop fusion | flops 7372800 | bytes 11796480 | tf_op jit(solution)/shard_map/convert_element_type | solution.py:124
  757.5 7.6 reshape.183
  765.2 7.1 multiply_reduce_fusion
  773.9 2.4 fusion.25
  (55 shorter events, 9.9 us)
Async XLA Ops:
  6.5 76.4 %copy-start.5 = (s32[16]{0:T(128)S(1)}, s32[16]{0:T(128)}, u32[]{:S(2)}) copy-start(s32[16]{0:T(128)} %param.17) | copy-start | bytes 196
  6.5 164.6 %all-gather.2.cloned.1.call-start = ((), (), s32[]{:S(2)}) async-start(), calls=%async_computation.2 | async-start | bytes 13271040 | tf_op jit(solution)/shard_map/all_gather | solution.py:88
  90.8 80.3 %copy-start.6 = (bf16[1,128,2880]{1,2,0:T(8,128)(2,1)S(1)}, bf16[1,128,2880]{1,2,0:T(8,128)(2,1)}, u32[]{:S(2)}) copy-start(bf16[1,128,2880]{1,2,0:T(8,128)(2,1)} %param.14) | copy-start | bytes 2211844
  171.1 7.4 copy-start.3
  177.3 1.2 copy-start.1
  296.0 151.5 %slice-start = ((s8[8478720]{0:T(1024)(128)(4,1)}), s8[4194304]{0:T(1024)(128)(4,1)S(1)}, s32[]{:S(2)}) async-start(s8[8478720]{0:T(1024)(128)(4,1)} %bitcast.83), calls=%async_computation.3 | async-start | bytes 8388608
  296.0 151.5 %slice-start.1 = ((s8[8478720]{0:T(1024)(128)(4,1)}), s8[4194304]{0:T(1024)(128)(4,1)S(1)}, s32[]{:S(2)}) async-start(s8[8478720]{0:T(1024)(128)(4,1)} %bitcast.83), calls=%async_computation.4 | async-start | bytes 8388608
  301.4 146.1 %slice-start.2 = ((s8[8478720]{0:T(1024)(128)(4,1)}), s8[90112]{0:T(1024)(128)(4,1)S(1)}, s32[]{:S(2)}) async-start(s8[8478720]{0:T(1024)(128)(4,1)} %bitcast.83), calls=%async_computation.5 | async-start | bytes 180224
  301.4 167.2 %slice-start.3 = ((s8[4239360]{0:T(1024)(128)(4,1)}), s8[4194304]{0:T(1024)(128)(4,1)S(1)}, s32[]{:S(2)}) async-start(s8[4239360]{0:T(1024)(128)(4,1)} %bitcast.85), calls=%async_computation.6 | async-start | bytes 8388608
  447.5 21.2 %slice-start.4 = ((s8[4239360]{0:T(1024)(128)(4,1)}), s8[45056]{0:T(1024)(128)(4,1)S(1)}, s32[]{:S(2)}) async-start(s8[4239360]{0:T(1024)(128)(4,1)} %bitcast.85), calls=%async_computation.7 | async-start | bytes 90112
  502.1 16.2 %copy-start.4 = (f32[1,128,4]{1,2,0:T(4,128)S(1)}, f32[1,128,4]{1,2,0:T(4,128)}, u32[]{:S(2)}) copy-start(f32[1,128,4]{1,2,0:T(4,128)} %param.19) | copy-start | bytes 6148
  502.1 189.3 %all-to-all-start.1 = ((bf16[128,16,2880]{2,1,0:T(8,128)(2,1)}), bf16[128,16,2880]{2,1,0:T(8,128)(2,1)}, u32[]{:S(2)}, u32[]{:S(2)}) async-start(bf16[128,16,2880]{2,1,0:T(8,128)(2,1)} %bitcast.72), calls=%async_computation.1 | async-start | bytes 24117248 | tf_op jit(solution)/shard_map/all_to_all | solution.py:113
  691.4 18.0 %copy-start = (s32[512,1]{0,1:T(1,128)S(1)}, s32[512,1]{0,1:T(1,128)}, u32[]{:S(2)}) copy-start(s32[512,1]{0,1:T(1,128)} %get-tuple-element.6) | copy-start | bytes 6148
  765.2 8.7 %copy-start.2 = (f32[128,2880]{0,1:T(8,128)S(1)}, f32[128,2880]{0,1:T(8,128)}, u32[]{:S(2)}) copy-start(f32[128,2880]{0,1:T(8,128)} %copy-done.1) | copy-start | bytes 4423684
Sparse Core Ops, SparseCore 0:
  9.5 161.5 all-gather.1
where the time goes:
time: 787 us; the launch traced here: 783 us
  waiting for transfers between devices  250 us (32%)
  blocking collectives  217 us (28%)
  local copies, waits for them, and re-layouts  192 us (24%)
  matrix products  50.8 us (6%)
  other arithmetic  42.7 us (5%)
  starting transfers between devices  16.2 us (2%)
  between operations  13.6 us (2%)
    all_to_all x1, waiting for transfers between devices, local(): lax.all_to_all(expert_half(flat_rows, gate_up_local, down_local).reshape(...  173 us
    all_to_all x1, blocking collectives, local(): lax.all_to_all(doubled, ('ctx', 'exp'), split_axis=0, concat_axis=0, tile...  146 us
    scatter x1, local copies, waits for them, and re-layouts, local(): jnp.zeros((experts, capacity, D), jnp.bfloat16).at[flat_ids, slot_index]  107 us
    all_gather x1, waiting for transfers between devices, local(): lax.all_gather(out_weight, 'ctx', axis=0, tiled=True)  76.3 us
    all_gather x1, blocking collectives, local(): value_section = lax.all_gather(value_matrix, 'ctx', axis=1, tiled=True)  36.4 us
    all_gather x1, blocking collectives, local(): key_section = lax.all_gather(key_rows, 'ctx', axis=1, tiled=True)  34.9 us
    convert_element_type x1, other arithmetic, local(): summed = (paired[:, 0].astype(jnp.float32) + paired[:, 1].astype(jnp.floa...  26.1 us
    gather x1, local copies, waits for them, and re-layouts, local(): paired = returned.reshape(experts, 2, capacity, D)[flat_ids, :, slot_index]  22 us
  transfers between devices with their start and end apart: 2, of which 2 were waited for; matrix products, arithmetic and copies ran while one was open for 2% of the time, Pallas kernels for 0%

commit v1 on v0

--- a/solution.py
+++ b/solution.py
@@ -2,6 +2,7 @@
 import jax.numpy as jnp
 from jax import lax
 from jax.sharding import PartitionSpec as P
+from jax.lax import all_gather
 
 D = 2880
 QUERY_HEADS = 32
@@ -53,8 +54,11 @@
         lax.axis_index("ctx") * token_count + jnp.arange(token_count, dtype=jnp.int32)
     )
     query_head_rows = queries[0].reshape(token_count, KEY_VALUE_HEADS, query_group_size, HEAD_SIZE)
-    key_section = lax.all_gather(key_rows, "ctx", axis=1, tiled=True)
-    value_section = lax.all_gather(value_matrix, "ctx", axis=1, tiled=True)
+    key_section, value_section = jnp.split(
+        all_gather(jnp.concatenate([key_rows, value_matrix], axis=0), "ctx", axis=1, tiled=True),
+        [key_rows.shape[0]],
+        axis=0,
+    )
     section_length = key_section.shape[1]
     key_pos = locate(jnp.arange(section_length, dtype=jnp.int32))
     row_maximum = jnp.full(

time: 787 us -> 829 us (1.053)
  waiting for transfers between devices: 250 us -> 360 us
  blocking collectives: 217 us -> 145 us
    all_gather x2 -> x0, blocking collectives: 71.3 us -> none  [the longest x1 36.4 us: local(): value_section = lax.all_gather(value_matrix, 'ctx', axis=1, tiled=True)]
    all_gather x1, waiting for transfers between devices: 76.3 us -> 144 us  [local(): lax.all_gather(out_weight, 'ctx', axis=0, tiled=True)]
    all_gather x0 -> x1, waiting for transfers between devices: none -> 42.1 us  [local(): all_gather(jnp.concatenate([key_rows, value_matrix], axis=0), 'ctx', axis...]
  transfers between devices with their start and end apart: 2 -> 3, of which waited for: 2 -> 3; matrix products, arithmetic and copies ran while one was open for 2% -> 2% of each run, Pallas kernels for 0% -> 0%
where the time goes in v1:
time: 829 us; the launch traced here: 825 us
  waiting for transfers between devices  360 us (43%)
  local copies, waits for them, and re-layouts  194 us (23%)
  blocking collectives  145 us (17%)
  matrix products  50.8 us (6%)
  other arithmetic  45.7 us (6%)
  starting transfers between devices  16.3 us (2%)
  between operations  13.6 us (2%)
    all_to_all x1, waiting for transfers between devices, local(): lax.all_to_all(expert_half(flat_rows, gate_up_local, down_local).reshape(...  173 us
    all_to_all x1, blocking collectives, local(): lax.all_to_all(doubled, ('ctx', 'exp'), split_axis=0, concat_axis=0, tile...  145 us
    all_gather x1, waiting for transfers between devices, local(): lax.all_gather(out_weight, 'ctx', axis=0, tiled=True)  144 us
    scatter x1, local copies, waits for them, and re-layouts, local(): jnp.zeros((experts, capacity, D), jnp.bfloat16).at[flat_ids, slot_index]  107 us
    all_gather x1, waiting for transfers between devices, local(): all_gather(jnp.concatenate([key_rows, value_matrix], axis=0), 'ctx', axis...  42.1 us
    convert_element_type x1, other arithmetic, local(): summed = (paired[:, 0].astype(jnp.float32) + paired[:, 1].astype(jnp.floa...  26.2 us
    gather x1, local copies, waits for them, and re-layouts, local(): paired = returned.reshape(experts, 2, capacity, D)[flat_ids, :, slot_index]  22 us
    dot_general x1, matrix products, expert_half(): gate_up_out = jnp.dot(routed, gate_up, preferred_element_type=jnp.float32)  21.2 us
  transfers between devices with their start and end apart: 3, of which 3 were waited for; matrix products, arithmetic and copies ran while one was open for 2% of the time, Pallas kernels for 0%

profile of v1, /device:TPU:36, one launch (start us, length us, event | category | flops | bytes accessed | tf_op | source)
XLA Modules:
  0.0 825.3 jit_solution(5507942562224787054)
XLA Ops:
  15.3 42.1 %all-gather.3.cloned.1.call-done = bf16[2,1024,256]{2,1,0:T(8,128)(2,1)} async-done(((bf16[2,128,256]{2,1,0:T(8,128)(2,1)}), bf16[2,1024,256]{2,1,0:T(8,128)(2,1)}) %all-gather.3.cloned.1.call-update) | async-done | bytes 1048592 | tf_op jit(solution)/shard_map/all_gather | solution.py:58
  59.1 2.4 fusion
  61.6 4.3 fusion.1
  65.9 4.0 divide_convert_fusion
  69.9 144.0 %all-gather.5.cloned.1.call-done = bf16[2048,2880]{0,1:T(8,128)(2,1)} async-done(((bf16[256,2880]{0,1:T(8,128)(2,1)}), bf16[2048,2880]{0,1:T(8,128)(2,1)}) %all-gather.5.cloned.1.call-update) | async-done | bytes 11796496 | tf_op jit(solution)/shard_map/all_gather | solution.py:92
  213.8 6.2 multiply_reduce_fusion.1
  222.0 2.4 broadcast_in_dim.80
  224.4 4.4 reshape.192
  228.8 3.0 broadcast_in_dim.79
  231.8 107.0 %scatter_fusion = bf16[64,16,2880]{2,1,0:T(8,128)(2,1)} fusion(bf16[64,16,2880]{2,1,0:T(8,128)(2,1)} %broadcast_in_dim.79, s32[512]{0:T(512)S(1)} %bitcast.74, bf16[512,2880]{1,0:T(8,128)(2,1)S(1)} %reshape.192), kind=kCustom, calls=%fused_computation.1 | custom fusion | bytes 8851456 | tf_op jit(solution)/shard_map/scatter | solution.py:109
  338.7 5.4 broadcast_in_dim.81
  344.2 145.4 %all_to_all.10 = bf16[128,16,2880]{2,1,0:T(8,128)(2,1)S(1)} all-to-all(bf16[128,16,2880]{2,1,0:T(8,128)(2,1)S(1)} %bitcast.73), channel_id=1, replica_groups=mesh['ctx'=8,'exp'=16] {'ctx','exp'}, dimensions={0} | all-to-all | bytes 23592960 | tf_op jit(solution)/shard_map/all_to_all | solution.py:115
  489.6 21.2 %fusion.3 = f32[2048,1440]{0,1:T(8,128)} fusion(bf16[2048,2880]{1,0:T(8,128)(2,1)S(1)} %bitcast.76, bf16[1,2880,1440]{1,2,0:T(8,128)(2,1)S(1)} %bitcast.84), kind=kOutput, calls=%fused_computation.8 | convolution fusion | flops 16986931200 | bytes 31887360 | tf_op jit(solution)/shard_map/dot_general | solution.py:17
  510.8 17.1 %convolution_convert_fusion = bf16[2048,2880]{0,1:T(8,128)(2,1)} fusion(bf16[1,720,2880]{2,1,0:T(8,128)(2,1)S(1)} %bitcast.86, f32[2048,1440]{0,1:T(8,128)} %fusion.3), kind=kOutput, calls=%fused_computation.7 | convolution fusion | flops 8511160320 | bytes 27740160 | tf_op jit(solution)/shard_map/dot_general | solution.py:23
  527.9 16.3 %copy.63 = bf16[2048,2880]{1,0:T(8,128)(2,1)} copy(bf16[2048,2880]{0,1:T(8,128)(2,1)} %convolution_convert_fusion) | data formatting | bytes 23592960 | tf_op jit(solution)/shard_map/convert_element_type | solution.py:23
  544.2 16.2 %all-to-all-start.1 = ((bf16[128,16,2880]{2,1,0:T(8,128)(2,1)}), bf16[128,16,2880]{2,1,0:T(8,128)(2,1)}, u32[]{:S(2)}, u32[]{:S(2)}) async-start(bf16[128,16,2880]{2,1,0:T(8,128)(2,1)} %bitcast.72), calls=%async_computation.1 | async-start | bytes 24117248 | tf_op jit(solution)/shard_map/all_to_all | solution.py:117
  560.6 172.9 %all-to-all-done.1 = bf16[128,16,2880]{2,1,0:T(8,128)(2,1)} async-done(((bf16[128,16,2880]{2,1,0:T(8,128)(2,1)}), bf16[128,16,2880]{2,1,0:T(8,128)(2,1)}, u32[]{:S(2)}, u32[]{:S(2)}) %all-to-all-start.1) | async-done | bytes 11796512 | tf_op jit(solution)/shard_map/all_to_all | solution.py:117
  733.5 18.0 %copy.64 = bf16[64,2,16,2880]{3,1,2,0:T(2,128)(2,1)} copy(bf16[64,2,16,2880]{3,2,1,0:T(8,128)(2,1)} %bitcast.20) | data formatting | bytes 23592960 | tf_op jit(solution)/shard_map/reshape | solution.py:124
  751.5 22.0 %gather_fusion = bf16[512,2,2880]{2,1,0:T(2,128)(2,1)} fusion(bf16[64,2,16,2880]{3,1,2,0:T(2,128)(2,1)} %copy.64, s32[512]{0:T(512)S(1)} %bitcast.75), kind=kCustom, calls=%fused_computation | custom fusion | bytes 11800576 | tf_op jit(solution)/shard_map/gather | solution.py:124
  773.6 26.2 %fusion.11 = f32[512,2880]{1,0:T(8,128)} fusion(bf16[512,2,2880]{2,1,0:T(2,128)(2,1)} %gather_fusion), kind=kLoop, calls=%fused_computation.16 | loop fusion | flops 7372800 | bytes 11796480 | tf_op jit(solution)/shard_map/convert_element_type | solution.py:128
  799.8 7.6 reshape.183
  807.4 7.1 multiply_reduce_fusion
  814.5 1.6 copy.66
  816.1 2.4 fusion.25
  (56 shorter events, 12.5 us)
Async XLA Ops:
  6.5 50.9 %all-gather.3.cloned.1.call-start = ((), (), s32[]{:S(2)}) async-start(), calls=%async_computation.2 | async-start | bytes 1179648 | tf_op jit(solution)/shard_map/all_gather | solution.py:58
  8.1 205.7 %all-gather.5.cloned.1.call-start = ((), (), s32[]{:S(2)}) async-start(), calls=%async_computation.3 | async-start | bytes 13271040 | tf_op jit(solution)/shard_map/all_gather | solution.py:92
  65.9 148.0 %copy-start.5 = (bf16[1,128,2880]{1,2,0:T(8,128)(2,1)S(1)}, bf16[1,128,2880]{1,2,0:T(8,128)(2,1)}, u32[]{:S(2)}) copy-start(bf16[1,128,2880]{1,2,0:T(8,128)(2,1)} %param.14) | copy-start | bytes 2211844
  213.8 7.4 copy-start.3
  220.0 1.2 copy-start.1
  338.7 150.8 %slice-start = ((s8[8478720]{0:T(1024)(128)(4,1)}), s8[4194304]{0:T(1024)(128)(4,1)S(1)}, s32[]{:S(2)}) async-start(s8[8478720]{0:T(1024)(128)(4,1)} %bitcast.83), calls=%async_computation.4 | async-start | bytes 8388608
  338.7 150.8 %slice-start.1 = ((s8[8478720]{0:T(1024)(128)(4,1)}), s8[4194304]{0:T(1024)(128)(4,1)S(1)}, s32[]{:S(2)}) async-start(s8[8478720]{0:T(1024)(128)(4,1)} %bitcast.83), calls=%async_computation.5 | async-start | bytes 8388608
  344.1 145.4 %slice-start.2 = ((s8[8478720]{0:T(1024)(128)(4,1)}), s8[90112]{0:T(1024)(128)(4,1)S(1)}, s32[]{:S(2)}) async-start(s8[8478720]{0:T(1024)(128)(4,1)} %bitcast.83), calls=%async_computation.6 | async-start | bytes 180224
  344.1 166.7 %slice-start.3 = ((s8[4239360]{0:T(1024)(128)(4,1)}), s8[4194304]{0:T(1024)(128)(4,1)S(1)}, s32[]{:S(2)}) async-start(s8[4239360]{0:T(1024)(128)(4,1)} %bitcast.85), calls=%async_computation.7 | async-start | bytes 8388608
  489.6 21.2 %slice-start.4 = ((s8[4239360]{0:T(1024)(128)(4,1)}), s8[45056]{0:T(1024)(128)(4,1)S(1)}, s32[]{:S(2)}) async-start(s8[4239360]{0:T(1024)(128)(4,1)} %bitcast.85), calls=%async_computation.8 | async-start | bytes 90112
  544.2 16.2 %copy-start.4 = (f32[1,128,4]{1,2,0:T(4,128)S(1)}, f32[1,128,4]{1,2,0:T(4,128)}, u32[]{:S(2)}) copy-start(f32[1,128,4]{1,2,0:T(4,128)} %param.19) | copy-start | bytes 6148
  544.2 189.3 %all-to-all-start.1 = ((bf16[128,16,2880]{2,1,0:T(8,128)(2,1)}), bf16[128,16,2880]{2,1,0:T(8,128)(2,1)}, u32[]{:S(2)}, u32[]{:S(2)}) async-start(bf16[128,16,2880]{2,1,0:T(8,128)(2,1)} %bitcast.72), calls=%async_computation.1 | async-start | bytes 24117248 | tf_op jit(solution)/shard_map/all_to_all | solution.py:117
  733.5 18.0 %copy-start = (s32[512,1]{0,1:T(1,128)S(1)}, s32[512,1]{0,1:T(1,128)}, u32[]{:S(2)}) copy-start(s32[512,1]{0,1:T(1,128)} %get-tuple-element.6) | copy-start | bytes 6148
  807.4 8.7 %copy-start.2 = (f32[128,2880]{0,1:T(8,128)S(1)}, f32[128,2880]{0,1:T(8,128)}, u32[]{:S(2)}) copy-start(f32[128,2880]{0,1:T(8,128)} %copy-done.1) | copy-start | bytes 4423684
Sparse Core Ops, SparseCore 0:
  9.7 47.6 all-gather.2
  59.6 154.1 all-gather.4
